TPU v7x, 32 devices: a whole 2x2x4 slice. The times are simulated.
32 devices in a mesh: seq: 8 (over z, x), batch: 4 (over y, core).
Axes of the slice: x: 2, y: 2, z: 4, core: 2. Of those that a mesh axis runs over, the one named last changes fastest.
Arguments:
- inputs: bfloat16 [32768, 768], P(('batch', 'seq')), parts along dimension 0, may hold values from -6 to 6
- token_rates: float32 [32768], P(('batch', 'seq')), parts along dimension 0, may hold values from 0.1 to 1
- proj_query: bfloat16 [768, 256], replicated, may hold values from -0.21875 to 0.21875
- proj_key: bfloat16 [768, 256], replicated, may hold values from -0.21875 to 0.21875
- proj_value: bfloat16 [768, 256], replicated, may hold values from -0.21875 to 0.21875
- proj_output: bfloat16 [256, 768], replicated, may hold values from -0.375 to 0.375
- fast_in: float32 [256, 512], replicated, may hold values from -0.375 to 0.375
- fast_up: float32 [256, 512], replicated, may hold values from -0.375 to 0.375
- fast_out: float32 [512, 256], replicated, may hold values from -0.25 to 0.25
- cotangent: bfloat16 [32768, 768], P(('batch', 'seq')), parts along dimension 0, may hold values from -6 to 6
Outputs:
- back_inputs: bfloat16 [32768, 768], P(('batch', 'seq')), parts along dimension 0
- back_rate: float32 [32768], P(('batch', 'seq')), parts along dimension 0
- grad_in: float32 [1024, 512], P('batch'), parts along dimension 0
- grad_up: float32 [1024, 512], P('batch'), parts along dimension 0
- grad_out: float32 [2048, 256], P('batch'), parts along dimension 0
- grad_query: float32 [768, 1024], P('seq', 'batch'), parts along dimension 1
- grad_key: float32 [768, 1024], P('seq', 'batch'), parts along dimension 1
- grad_value: float32 [768, 1024], P('seq', 'batch'), parts along dimension 1
- grad_output: float32 [1024, 768], P('batch', 'seq'), parts along dimension 0
There are 4 independent parts, one for each index of `batch`. A program takes and returns all parts, laid end to end along the dimension named above; an argument that names none is the same for every part. Nothing has to cross between parts.
All inputs are finite; a program needn't handle non-finite values.
Results may differ from a plain program's by a relative error of at most 0.029.
Values may be sent and summed in bfloat16 or wider, within the bound.
A program may use at most 128 MiB of HBM per device.

v0:
```python
import functools
import math

import jax
import jax.numpy as jnp
from jax import lax
from jax.experimental import pallas as pl
from jax.experimental.pallas import tpu as pltpu
from jax.sharding import PartitionSpec as P

NS_STEPS = 5
C1, C3, C5 = 3.4445, -4.775, 2.0315
EPS = 1e-07
MESH = pl.DeviceIdType.MESH
VMEM_LIMIT = 60 * 1024 * 1024
PAIR = 2
PASSES_FWD = 3
PASSES_BWD = 3


def rounded(value):
    return value.astype(jnp.bfloat16)


def product(left, right):
    return jnp.dot(left, right, preferred_element_type=jnp.float32)


def token_sum(left, right):
    return lax.dot_general(
        left, right, (((0,), (0,)), ((), ())), preferred_element_type=jnp.float32
    )


def times_transpose(left, right):
    return lax.dot_general(
        left, right, (((1,), (1,)), ((), ())), preferred_element_type=jnp.float32
    )


def silu_parts(pre_act):
    sigma_val = jax.nn.sigmoid(pre_act)
    activation = pre_act * sigma_val
    slope_val = sigma_val * (1.0 + pre_act * (1.0 - sigma_val))
    curvature = sigma_val * (1.0 - sigma_val) * (2.0 + pre_act * (1.0 - 2.0 * sigma_val))
    return (activation, slope_val, curvature)


def split(value, passes):
    high = rounded(value)
    if passes == 1:
        return (high,)
    return (high, rounded(value - high.astype(jnp.float32)))


def dot_split(left, right, dot):
    if len(left) == 1:
        return dot(left[0], right[0])
    along = 1 if dot is times_transpose else 0
    return dot(
        jnp.concatenate([left[0], left[0], left[1]], axis=1),
        jnp.concatenate([right[0], right[1], right[0]], axis=along),
    )


def ns_start(totals, xs):
    norms = []
    for m, matrix in enumerate(totals):
        norm = jnp.sqrt(jnp.sum(matrix * matrix))
        norms.append(norm)
        xs[0, m] = matrix / (norm + EPS)
    return norms


def ns_forward(first, last, xs, grams, polys, count, passes):
    each = range(count)

    def step(k, carry):
        xparts = [split(xs[k, m], passes) for m in each]
        gram = [dot_split(xparts[m], xparts[m], times_transpose) for m in each]
        gparts = [split(gram[m], passes) for m in each]
        poly = [C3 * gram[m] + C5 * dot_split(gparts[m], gparts[m], product) for m in each]
        pparts = [split(poly[m], passes) for m in each]
        for m in each:
            if grams is not None:
                grams[k, m] = gram[m]
                polys[k, m] = poly[m]
            xs[k + 1, m] = C1 * xs[k, m] + dot_split(pparts[m], xparts[m], product)
        return carry

    lax.fori_loop(first, last, step, 0)


def ns_backward(first, last, xs, grams, polys, grads, count, passes):
    each = range(count)

    def step(i, carry):
        k = NS_STEPS - 1 - i
        gparts = [split(grads[m], passes) for m in each]
        xparts = [split(xs[k, m], passes) for m in each]
        dpoly = [dot_split(gparts[m], xparts[m], times_transpose) for m in each]
        sym = [dpoly[m] + dpoly[m].T for m in each]
        twist = [
            dot_split(split(sym[m], passes), split(grams[k, m], passes), product) for m in each
        ]
        weight = [C3 * sym[m] + C5 * (twist[m] + twist[m].T) for m in each]
        for m in each:
            grads[m] = (
                C1 * grads[m]
                + dot_split(split(polys[k, m], passes), gparts[m], product)
                + dot_split(split(weight[m], passes), xparts[m], product)
            )
        return carry

    lax.fori_loop(first, last, step, 0)


def ns_finish(totals, norms, grads, count):
    out = []
    for m in range(count):
        shifted = norms[m] + EPS
        dot_all = jnp.sum(grads[m] * totals[m])
        out.append(grads[m] / shifted - totals[m] * (dot_all / (norms[m] * shifted * shifted)))
    return out


def place():
    me = lax.axis_index("seq")
    return me // PAIR, me % PAIR


def remote(src, dst, send, recv, device):
    copy = pltpu.make_async_remote_copy(
        src_ref=src,
        dst_ref=dst,
        send_sem=send,
        recv_sem=recv,
        device_id={"seq": device},
        device_id_type=MESH,
    )
    copy.start()
    return copy


def line_peer(lines, d):
    line, side = place()
    return lax.rem(line + d, lines) * PAIR + side


def partner():
    line, side = place()
    return line * PAIR + (1 - side)


def greet(lines):
    barrier = pltpu.get_barrier_semaphore()
    for peer in [partner()] + [line_peer(lines, d) for d in range(1, lines)]:
        pl.semaphore_signal(barrier, inc=1, device_id={"seq": peer}, device_id_type=MESH)
    pl.semaphore_wait(barrier, lines)


def start_pairs(lines, src, buf):
    line, side = place()
    copies = []
    for d in list(range(1, lines)) + [0]:
        to = lax.rem(line + d, lines)
        copies.append(
            remote(
                src.at[to * PAIR + (1 - side)],
                buf.paired.at[d],
                buf.sems.at[0, d],
                buf.sems.at[1, d],
                partner(),
            )
        )
    return copies


def forward_pairs(lines, src, buf, copies, first=1, last=None):
    line, side = place()
    sent = []
    for d in range(lines if last is None else last)[first:]:
        copy = copies[d - 1]
        to = lax.rem(line + d, lines)
        copy.wait()
        buf.middle[d] = rounded(
            src[to * PAIR + side].astype(jnp.float32) + buf.paired[d].astype(jnp.float32)
        )
        sent.append(
            remote(
                buf.middle.at[d],
                buf.lined.at[d],
                buf.sems.at[2, d],
                buf.sems.at[3, d],
                to * PAIR + side,
            )
        )
    return sent


def finish_scatter(lines, src, buf, copies, sent):
    copies[-1].wait()
    total = src[lax.axis_index("seq")].astype(jnp.float32) + buf.paired[0].astype(jnp.float32)
    for d, copy in zip(range(1, lines), sent):
        copy.wait()
        total = total + buf.lined[d].astype(jnp.float32)
    return total


def start_gather(lines, buf):
    out = []
    for d in range(1, lines):
        out.append(
            remote(
                buf.mine,
                buf.gathered.at[d],
                buf.sems.at[4, d],
                buf.sems.at[5, d],
                line_peer(lines, d),
            )
        )
    across = remote(buf.mine, buf.crossed.at[0], buf.sems.at[6, 0], buf.sems.at[7, 0], partner())
    return out, [across]


def relay_gather(lines, buf, copies):
    out, across = copies
    for d in range(1, lines):
        out[d - 1].wait()
        across.append(
            remote(
                buf.gathered.at[d],
                buf.crossed.at[d],
                buf.sems.at[6, d],
                buf.sems.at[7, d],
                partner(),
            )
        )


def finish_gather(lines, buf, copies, full):
    line, side = place()
    rows = buf.mine.shape[0]
    across = copies[1]

    def put(owner, block):
        full[pl.ds(pl.multiple_of(owner * rows, rows), rows), :] = block.astype(jnp.float32)

    put(line * PAIR + side, buf.mine[...])
    for d in range(1, lines):
        put(lax.rem(line - d + lines, lines) * PAIR + side, buf.gathered[d])
    for d in range(lines):
        across[d].wait()
        put(lax.rem(line - d + lines, lines) * PAIR + (1 - side), buf.crossed[d])


class Scatter:
    def __init__(self, paired, middle, lined, sems):
        self.paired, self.middle, self.lined, self.sems = paired, middle, lined, sems

    @staticmethod
    def scratch(lines, block):
        slots = pltpu.VMEM((lines,) + block, jnp.bfloat16)
        return [slots, slots, slots, pltpu.SemaphoreType.DMA((4, lines))]


class Reduce(Scatter):
    def __init__(self, paired, middle, lined, mine, gathered, crossed, sems):
        super().__init__(paired, middle, lined, sems)
        self.mine, self.gathered, self.crossed = mine, gathered, crossed

    @staticmethod
    def scratch(lines, block):
        slots = pltpu.VMEM((lines,) + block, jnp.bfloat16)
        one = pltpu.VMEM(block, jnp.bfloat16)
        return [slots, slots, slots, one, slots, slots, pltpu.SemaphoreType.DMA((8, lines))]


def forward_kernel(
    lines, count, part, fast_in, fast_up, fast_out, inputs, proj_query, cotangent, proj_output,
    n_in, n_up, n_out, total_out, query_rows, back_output, *scratch
):
    buf, xs = Reduce(*scratch[:7]), scratch[7]
    greet(lines)
    copies = start_pairs(lines, part, buf)
    query_rows[...] = rounded(product(inputs[...], proj_query[...]))
    back_output[...] = rounded(times_transpose(cotangent[...], proj_output[...]))
    sent = forward_pairs(lines, part, buf, copies)
    buf.mine[...] = rounded(finish_scatter(lines, part, buf, copies, sent))
    gathering = start_gather(lines, buf)
    relay_gather(lines, buf, gathering)
    finish_gather(lines, buf, gathering, total_out)
    h = total_out.shape[0] // count
    totals = [total_out[m * h : (m + 1) * h, :] for m in range(count)]
    ns_start(totals, xs)
    ns_forward(0, NS_STEPS, xs, None, None, count, PASSES_FWD)
    n_in[...] = rounded(fast_in[...] + xs[NS_STEPS, 0])
    n_up[...] = rounded(fast_up[...] + xs[NS_STEPS, 1])
    n_out[...] = rounded(fast_out[...] + xs[NS_STEPS, 2].T)


def fill_rows(rows_part, pairs):
    n, rows = rows_part.shape[:2]
    at = 0
    for left, right in pairs:
        total = token_sum(left[...], right[...])
        wide = total.shape[1]
        for j in range(n):
            rows_part[j, :, at : at + wide] = rounded(total[j * rows : (j + 1) * rows, :])
        at += wide


def backward_kernel(
    lines, count, part, inputs, query_grad, cotangent, output_rows, total_ref,
    adjoint_out, back_out, rows_out, *scratch
):
    buf, row_buf = Reduce(*scratch[:7]), Scatter(*scratch[7:11])
    rows_part, xs, grams, polys, grads = scratch[11:]
    greet(lines)
    copies = start_pairs(lines, part, buf)
    h = total_ref.shape[0] // count
    totals = [total_ref[m * h : (m + 1) * h, :] for m in range(count)]
    norms = ns_start(totals, xs)
    fill_rows(rows_part, ((inputs, query_grad), (cotangent, output_rows)))
    sent = forward_pairs(lines, part, buf, copies, 1, lines - 1)
    ns_forward(0, NS_STEPS - 4, xs, grams, polys, count, PASSES_FWD)
    sent += forward_pairs(lines, part, buf, copies, lines - 1)
    ns_forward(NS_STEPS - 4, NS_STEPS - 2, xs, grams, polys, count, PASSES_FWD)
    buf.mine[...] = rounded(finish_scatter(lines, part, buf, copies, sent))
    gathering = start_gather(lines, buf)
    ns_forward(NS_STEPS - 2, NS_STEPS - 1, xs, grams, polys, count, PASSES_FWD)
    relay_gather(lines, buf, gathering)
    ns_forward(NS_STEPS - 1, NS_STEPS, xs, grams, polys, count, PASSES_FWD)
    finish_gather(lines, buf, gathering, adjoint_out)
    copies = start_pairs(lines, rows_part, row_buf)
    for m in range(count):
        grads[m] = adjoint_out[m * h : (m + 1) * h, :]
    ns_backward(0, NS_STEPS - 2, xs, grams, polys, grads, count, PASSES_BWD)
    sent = forward_pairs(lines, rows_part, row_buf, copies)
    ns_backward(NS_STEPS - 2, NS_STEPS, xs, grams, polys, grads, count, PASSES_BWD)
    result = ns_finish(totals, norms, grads, count)
    for m in range(count):
        back_out[m * h : (m + 1) * h, :] = rounded(result[m])
    rows_out[...] = finish_scatter(lines, rows_part, row_buf, copies, sent)


def final_kernel(
    lines, count, part, inputs, query_grad, key_grad, value_grad,
    proj_query, proj_key, proj_value, adjoint,
    grad_in, grad_up, grad_out, grad_key, grad_value, back_inputs, *scratch
):
    buf, row_buf = Reduce(*scratch[:7]), Scatter(*scratch[7:11])
    rows_part, total = scratch[11:]
    greet(lines)
    copies = start_pairs(lines, part, buf)
    fill_rows(rows_part, ((inputs, key_grad), (inputs, value_grad)))
    row_copies = start_pairs(lines, rows_part, row_buf)
    sent = forward_pairs(lines, part, buf, copies)
    buf.mine[...] = rounded(finish_scatter(lines, part, buf, copies, sent))
    gathering = start_gather(lines, buf)
    row_sent = forward_pairs(lines, rows_part, row_buf, row_copies)
    relay_gather(lines, buf, gathering)

    tile = math.gcd(inputs.shape[0], 256)
    weights = jnp.concatenate([proj_query[...], proj_key[...], proj_value[...]], axis=1)

    def tokens(i, carry):
        at = pl.ds(pl.multiple_of(i * tile, tile), tile)
        grads = jnp.concatenate([query_grad[at, :], key_grad[at, :], value_grad[at, :]], axis=1)
        back_inputs[at, :] = rounded(times_transpose(grads, weights))
        return carry

    lax.fori_loop(0, inputs.shape[0] // tile, tokens, 0)
    sums = finish_scatter(lines, rows_part, row_buf, row_copies, row_sent)
    h = key_grad.shape[1]
    grad_key[...] = sums[:, :h]
    grad_value[...] = sums[:, h:]
    finish_gather(lines, buf, gathering, total)
    grad_in[...] = adjoint[:h, :] + total[:h, :]
    grad_up[...] = adjoint[h : 2 * h, :] + total[h : 2 * h, :]
    grad_out[...] = (adjoint[2 * h :, :] + total[2 * h :, :]).T


def call(kernel, identity, outs, scratch, *operands):
    vmem = pl.BlockSpec(memory_space=pltpu.VMEM)
    return pl.pallas_call(
        kernel,
        out_shape=[jax.ShapeDtypeStruct(s, d) for s, d in outs],
        in_specs=[vmem] * len(operands),
        out_specs=[vmem] * len(outs),
        scratch_shapes=scratch,
        compiler_params=pltpu.CompilerParams(
            collective_id=identity, has_side_effects=True, vmem_limit_bytes=VMEM_LIMIT
        ),
    )(*operands)


def body(
    n,
    inputs,
    token_rates,
    proj_query,
    proj_key,
    proj_value,
    proj_output,
    fast_in,
    fast_up,
    fast_out,
    cotangent,
):
    bf16, f32 = jnp.bfloat16, jnp.float32
    h, f = fast_in.shape
    width = inputs.shape[1]
    count = 3
    block = (count * h // n, f)
    row_block = (width // n, 2 * h)

    key_rows = rounded(product(inputs, proj_key))
    value_rows = rounded(product(inputs, proj_value))
    w_in, w_up, w_out = (rounded(fast_in), rounded(fast_up), rounded(fast_out))
    scaled = rounded(token_rates[:, None] * value_rows.astype(f32))
    pre_in = product(key_rows, w_in)
    pre_up = product(key_rows, w_up)
    activation, slope_val, curvature = silu_parts(pre_in)
    hidden = rounded(activation * pre_up)
    upstream = times_transpose(scaled, w_out)
    grad_in_rows = rounded(upstream * pre_up * slope_val)
    grad_up_rows = rounded(upstream * activation)

    def stacked(*terms):
        return jnp.concatenate([rounded(t) for t in terms]).reshape((n,) + block)

    part = stacked(
        token_sum(key_rows, grad_in_rows),
        token_sum(key_rows, grad_up_rows),
        token_sum(scaled, hidden),
    )
    lines = n // PAIR
    exchange = Reduce.scratch(lines, block)
    row_scratch = Scatter.scratch(lines, row_block)
    n_in, n_up, n_out, totals, query_rows, back_output = call(
        functools.partial(forward_kernel, lines, count),
        0,
        [
            ((h, f), bf16),
            ((h, f), bf16),
            ((f, h), bf16),
            ((count * h, f), f32),
            ((inputs.shape[0], h), bf16),
            ((inputs.shape[0], h), bf16),
        ],
        exchange + [pltpu.VMEM((NS_STEPS + 1, count, h, f), f32)],
        part, fast_in, fast_up, fast_out, inputs, proj_query, cotangent, proj_output,
    )

    pre_p = product(query_rows, n_in)
    pre_r = product(query_rows, n_up)
    activation_q, slope_q, _ = silu_parts(pre_p)
    hidden_q = rounded(activation_q * pre_r)
    output_rows = rounded(product(hidden_q, n_out))
    back_hidden = times_transpose(back_output, n_out)
    back_p = rounded(back_hidden * pre_r * slope_q)
    back_r = rounded(back_hidden * activation_q)
    query_grad = rounded(times_transpose(back_p, n_in) + times_transpose(back_r, n_up))
    part = stacked(
        token_sum(query_rows, back_p),
        token_sum(query_rows, back_r),
        token_sum(back_output, hidden_q),
    )
    adjoint, back_totals, rows_sum = call(
        functools.partial(backward_kernel, lines, count),
        1,
        [((count * h, f), f32), ((count * h, f), bf16), (row_block, f32)],
        exchange
        + row_scratch
        + [
            pltpu.VMEM((n,) + row_block, bf16),
            pltpu.VMEM((NS_STEPS + 1, count, h, f), f32),
            pltpu.VMEM((NS_STEPS, count, h, h), f32),
            pltpu.VMEM((NS_STEPS, count, h, h), f32),
            pltpu.VMEM((count, h, f), f32),
        ],
        part, inputs, query_grad, cotangent, output_rows, totals,
    )
    grad_query = rows_sum[:, :h]
    grad_output = rows_sum[:, h:].T

    b_in, b_up, b_out = (back_totals[m * h : (m + 1) * h] for m in range(count))
    press_in = product(key_rows, b_in)
    press_up = product(key_rows, b_up)
    back_hid = product(scaled, b_out)
    back_upstream = rounded(press_in * pre_up * slope_val + press_up * activation)
    back_pre_up = rounded(press_in * upstream * slope_val + back_hid * activation)
    back_pre_in = rounded(
        press_in * upstream * pre_up * curvature
        + press_up * upstream * slope_val
        + back_hid * pre_up * slope_val
    )
    back_scaled = times_transpose(hidden, b_out) + product(back_upstream, w_out)
    back_rate = jnp.sum(back_scaled * value_rows.astype(f32), axis=1)
    key_sum = times_transpose(grad_in_rows, b_in) + times_transpose(grad_up_rows, b_up)
    key_sum = key_sum + times_transpose(back_pre_in, w_in) + times_transpose(back_pre_up, w_up)
    key_grad = rounded(key_sum)
    value_grad = rounded(token_rates[:, None] * back_scaled)
    part = stacked(
        token_sum(key_rows, back_pre_in),
        token_sum(key_rows, back_pre_up),
        token_sum(scaled, back_upstream),
    )
    grad_in, grad_up, grad_out, grad_key, grad_value, back_inputs = call(
        functools.partial(final_kernel, lines, count),
        2,
        [
            ((h, f), f32),
            ((h, f), f32),
            ((f, h), f32),
            ((width // n, h), f32),
            ((width // n, h), f32),
            (inputs.shape, bf16),
        ],
        exchange
        + row_scratch
        + [pltpu.VMEM((n,) + row_block, bf16), pltpu.VMEM((count * h, f), f32)],
        part, inputs, query_grad, key_grad, value_grad,
        proj_query, proj_key, proj_value, adjoint,
    )
    return (
        back_inputs,
        back_rate,
        grad_in,
        grad_up,
        grad_out,
        grad_query,
        grad_key,
        grad_value,
        grad_output,
    )


def solution(mesh):
    in_specs = (
        P(("batch", "seq"), None),
        P(("batch", "seq")),
        P(),
        P(),
        P(),
        P(),
        P(),
        P(),
        P(),
        P(("batch", "seq"), None),
    )
    out_specs = (
        P(("batch", "seq"), None),
        P(("batch", "seq")),
        P("batch", None),
        P("batch", None),
        P("batch", None),
        P("seq", "batch"),
        P("seq", "batch"),
        P("seq", "batch"),
        P("batch", "seq"),
    )
    return jax.shard_map(
        functools.partial(body, mesh.shape["seq"]),
        mesh=mesh,
        in_specs=in_specs,
        out_specs=out_specs,
        check_vma=False,
    )
```

profile of v0, /device:TPU:0, one launch (start us, length us, event | category | flops | bytes accessed | tf_op | source)
XLA Modules:
  0.0 174.1 jit_solution(8901212197997865078)
XLA Ops:
  0.7 2.2 %convolution_convert_fusion.2 = bf16[1024,256]{1,0:T(8,128)(2,1)S(1)} fusion(bf16[1024,768]{1,0:T(8,128)(2,1)} %inputs.5, bf16[768,256]{1,0:T(8,128)(2,1)} %proj_key.1), kind=kOutput, calls=%fused_computation.32 | convolution fusion | flops 402915328 | bytes 2490368 | tf_op jit(solution)/shard_map/dot_general | solution.py:26
  2.9 0.6 convolution_convert_fusion.1
  3.9 0.6 copy-done.3
  5.0 1.0 copy-done.6
  5.9 2.6 %multiply_convert_fusion.5 = (bf16[1024,512]{1,0:T(8,128)(2,1)S(1)}, bf16[1024,512]{1,0:T(8,128)(2,1)S(1)}, bf16[1024,512]{1,0:T(8,128)(2,1)S(1)}, f32[1024,512]{1,0:T(8,128)}) fusion(f32[1024,512]{1,0:T(8,128)S(1)} %fusion.28, f32[1024,512]{1,0:T(8,128)S(1)} %fusion.25, f32[512,256]{1,0:T(8,128)S(1)} %copy-done.6, ...), kind=kOutput, calls=%fused_computation.18 | convolution fusion | flops 277217280 | bytes 10489856 | tf_op jit(solution)/shard_map/dot_general | solution.py:36
  9.0 0.8 convolution_convert_fusion.9
  10.3 0.9 pad_maximum_fusion
  11.3 44.1 %shard_map.169 = (bf16[256,512]{1,0:T(8,128)(2,1)}, bf16[256,512]{1,0:T(8,128)(2,1)}, bf16[512,256]{1,0:T(8,128)(2,1)}, f32[768,512]{1,0:T(8,128)}, bf16[1024,25...) custom-call(bf16[8,96,512]{2,1,0:T(8,128)(2,1)} %bitcast.49, f32[256,512]{1,0:T(8,128)} %fast_in.1, f32[256,512]{1,0:T(8,128)} %fast_up.1, ...), custom_call_target="tpu_custom_call" | custom-call | tf_op jit(solution)/shard_map/pallas_call | solution.py:386
  55.3 1.6 fusion.37
  57.4 0.5 copy-done.24
  58.0 1.4 multiply_convert_fusion.2
  60.7 1.3 fusion.9.query_grad
  62.4 0.9 pad_maximum_fusion.1
  63.4 1.2 convolution_convert_fusion.output_rows
  64.6 53.6 %shard_map.170 = (f32[768,512]{1,0:T(8,128)}, bf16[768,512]{1,0:T(8,128)(2,1)}, f32[96,512]{1,0:T(8,128)}) custom-call(bf16[8,96,512]{2,1,0:T(8,128)(2,1)} %bitcast.48, bf16[1024,768]{1,0:T(8,128)(2,1)} %inputs.5, bf16[1024,256]{1,0:T(8,128)(2,1)} %fusion.9.query_grad, bf16[1024,768]{1,0:T(8,128)(2,1)} %cotangent.3, ...), custom_call_target="tpu_custom_call" | custom-call | tf_op jit(solution)/shard_map/pallas_call | solution.py:386
  118.3 1.5 fusion.20
  120.8 0.7 slice_bitcast_fusion
  122.4 0.8 copy-done.11
  123.2 0.6 copy-done.9
  123.8 2.8 %fusion.6 = (bf16[1024,512]{1,0:T(8,128)(2,1)S(1)}, bf16[1024,512]{1,0:T(8,128)(2,1)S(1)}, bf16[1024,512]{1,0:T(8,128)(2,1)S(1)}) fusion(f32[1024,512]{1,0:T(8,128)S(1)} %copy-done.11, f32[1024,512]{1,0:T(8,128)S(1)} %fusion.18, f32[1024,512]{1,0:T(8,128)S(1)} %copy-done.29, f32[1024,512]{1,0:T(8,128)S(1)} %copy-done.9, f32[1024,512]{1,0:T(8,128)S(1)} %fusion.22, ...), kind=kOutput, calls=%fused_computation.8 | convolution fusion | flops 286523392 | bytes 14422016 | tf_op jit(solution)/shard_map/dot_general | solution.py:26
  126.7 1.8 %fusion.12 = (f32[1024]{0:T(1024)}, bf16[1024,256]{1,0:T(8,128)(2,1)}) fusion(bf16[1024,256]{1,0:T(8,128)(2,1)S(1)} %convolution_convert_fusion.1, f32[1024]{0:T(1024)S(1)} %copy-done.28, f32[1024,256]{1,0:T(8,128)S(1)} %fusion.13, bf16[1024,512]{1,0:T(8,128)(2,1)S(1)} %get-tuple-element.40, f32[512,256]{1,0:T(8,128)S(1)} %copy-done.7), kind=kOutput, calls=%fused_computation.43 | convolution fusion | flops 270138368 | bytes 3678208 | tf_op jit(solution)/shard_map/dot_general | solution.py:26
  128.5 0.8 convolution_convert_fusion.3
  129.3 0.5 convolution_add_fusion.2
  130.4 1.3 fusion.10.key_grad
  132.1 0.9 pad_maximum_fusion.2
  133.0 34.6 %shard_map.171 = (f32[256,512]{1,0:T(8,128)}, f32[256,512]{1,0:T(8,128)}, f32[512,256]{1,0:T(8,128)}, f32[96,256]{1,0:T(8,128)}, f32[96,256]{1,0:T(8,128)}, /*index=5*/bf16[1024,768]{1,0:T(8,128)(2,1)}) custom-call(bf16[8,96,512]{2,1,0:T(8,128)(2,1)} %bitcast.47, bf16[1024,768]{1,0:T(8,128)(2,1)} %inputs.5, bf16[1024,256]{1,0:T(8,128)(2,1)} %fusion.9.query_grad, ...), custom_call_target="tpu_custom_call" | custom-call | tf_op jit(solution)/shard_map/pallas_call | solution.py:386
  167.7 2.8 %copy.31 = bf16[1024,768]{1,0:T(8,128)(2,1)} copy(bf16[1024,768]{1,0:T(8,128)(2,1)} %get-tuple-element.62) | data formatting | bytes 3145728
  170.4 0.8 copy.32
  171.2 0.8 copy.33
  172.0 0.8 copy.34
  172.8 0.6 copy.35
  173.5 0.6 copy.36
  (70 shorter events, 7.0 us)
Async XLA Ops:
  0.6 2.2 %copy-start = (bf16[1024,768]{1,0:T(8,128)(2,1)S(1)}, bf16[1024,768]{1,0:T(8,128)(2,1)}, u32[]{:S(2)}) copy-start(bf16[1024,768]{1,0:T(8,128)(2,1)} %inputs.5) | copy-start | bytes 4718596
  0.7 2.8 %copy-start.1 = (f32[256,512]{1,0:T(8,128)S(1)}, f32[256,512]{1,0:T(8,128)}, u32[]{:S(2)}) copy-start(f32[256,512]{1,0:T(8,128)} %fast_in.1) | copy-start | bytes 1572868
  0.7 2.2 %copy-start.23 = (bf16[768,256]{1,0:T(8,128)(2,1)S(1)}, bf16[768,256]{1,0:T(8,128)(2,1)}, u32[]{:S(2)}) copy-start(bf16[768,256]{1,0:T(8,128)(2,1)} %proj_value.1) | copy-start | bytes 1179652
  3.5 1.0 copy-start.3
  4.5 4.0 %copy-start.8 = (f32[1024,512]{1,0:T(8,128)}, f32[1024,512]{1,0:T(8,128)S(1)}, u32[]{:S(2)}) copy-start(f32[1024,512]{1,0:T(8,128)S(1)} %fusion.25) | copy-start | bytes 6291460
  4.5 1.4 copy-start.6
  4.5 1.4 copy-start.28
  5.9 2.6 %copy-start.10 = (f32[1024,512]{1,0:T(8,128)}, f32[1024,512]{1,0:T(8,128)S(1)}, u32[]{:S(2)}) copy-start(f32[1024,512]{1,0:T(8,128)S(1)} %fusion.28) | copy-start | bytes 6291460
  8.5 1.3 copy-start.12
  8.6 1.3 copy-start.14
  55.3 1.7 copy-start.17
  55.3 1.7 copy-start.21
  57.0 1.0 copy-start.24
  57.9 1.4 copy-start.22
  62.0 1.4 copy-start.16
  64.6 53.7 %copy-start.15 = (bf16[1024,512]{1,0:T(8,128)(2,1)S(1)}, bf16[1024,512]{1,0:T(8,128)(2,1)}, u32[]{:S(2)}) copy-start(bf16[1024,512]{1,0:T(8,128)(2,1)} %copy-done.14) | copy-start | bytes 3145732
  118.2 1.6 copy-start.5
  118.3 1.6 copy-start.13
  119.8 1.0 copy-start.25
  120.3 2.1 %copy-start.29 = (f32[1024,512]{1,0:T(8,128)S(1)}, f32[1024,512]{1,0:T(8,128)}, u32[]{:S(2)}) copy-start(f32[1024,512]{1,0:T(8,128)} %get-tuple-element.52) | copy-start | bytes 6291460
  121.5 1.7 copy-start.11
  121.9 1.9 %copy-start.9 = (f32[1024,512]{1,0:T(8,128)S(1)}, f32[1024,512]{1,0:T(8,128)}, u32[]{:S(2)}) copy-start(f32[1024,512]{1,0:T(8,128)} %copy-done.8) | copy-start | bytes 6291460
  123.8 2.9 %copy-start.7 = (f32[512,256]{1,0:T(8,128)S(1)}, f32[512,256]{1,0:T(8,128)}, u32[]{:S(2)}) copy-start(f32[512,256]{1,0:T(8,128)} %fast_out.1) | copy-start | bytes 1572868
  126.7 2.6 %copy-start.2 = (f32[256,512]{1,0:T(8,128)S(1)}, f32[256,512]{1,0:T(8,128)}, u32[]{:S(2)}) copy-start(f32[256,512]{1,0:T(8,128)} %fast_in.1) | copy-start | bytes 1572868
  129.3 1.0 copy-start.4
  167.6 2.8 %copy-start.20 = (f32[256,512]{1,0:T(8,128)S(1)}, f32[256,512]{1,0:T(8,128)}, u32[]{:S(2)}) copy-start(f32[256,512]{1,0:T(8,128)} %get-tuple-element.64) | copy-start | bytes 1572868
  167.6 3.6 %copy-start.19 = (f32[256,512]{1,0:T(8,128)S(1)}, f32[256,512]{1,0:T(8,128)}, u32[]{:S(2)}) copy-start(f32[256,512]{1,0:T(8,128)} %get-tuple-element.65) | copy-start | bytes 1572868
  167.6 4.4 %copy-start.18 = (f32[512,256]{1,0:T(8,128)S(1)}, f32[512,256]{1,0:T(8,128)}, u32[]{:S(2)}) copy-start(f32[512,256]{1,0:T(8,128)} %get-tuple-element.66) | copy-start | bytes 1572868
  170.4 2.4 %copy-start.27 = (f32[96,256]{1,0:T(8,128)S(1)}, f32[96,256]{1,0:T(8,128)}, u32[]{:S(2)}) copy-start(f32[96,256]{1,0:T(8,128)} %get-tuple-element.68) | copy-start | bytes 294916
  170.4 3.0 %copy-start.26 = (f32[96,256]{1,0:T(8,128)S(1)}, f32[96,256]{1,0:T(8,128)}, u32[]{:S(2)}) copy-start(f32[96,256]{1,0:T(8,128)} %get-tuple-element.69) | copy-start | bytes 294916
where the time goes:
time: 174 us
  Pallas kernels  132 us (76%)
  matrix products  27.1 us (16%)
  local copies, waits for them, and re-layouts  10.9 us (6%)
  other arithmetic  2.79 us (2%)
    pallas_call x3, Pallas kernels, call(): pl.pallas_call(kernel, out_shape=[jax.ShapeDtypeStruct(s, d) for s, d in...  132 us
    dot_general x11, matrix products, product(): return jnp.dot(left, right, preferred_element_type=jnp.float32)  12.2 us
    unnamed x66, local copies, waits for them, and re-layouts  10.2 us
    dot_general x9, matrix products, times_transpose(): lax.dot_general(left, right, (((1,), (1,)), ((), ())), preferred_element_...  10.2 us
    dot_general x9, matrix products, token_sum(): lax.dot_general(left, right, (((0,), (0,)), ((), ())), preferred_element_...  4.71 us

commit v1 on v0

v1 whole, which is shorter than its diff:
```python
import functools
import math
from types import SimpleNamespace

import jax
import jax.numpy as jnp
from jax import lax
from jax.experimental import pallas as pl
from jax.experimental.pallas import tpu as pltpu
from jax.sharding import PartitionSpec as P

NS_STEPS = 5
NS_SINGLE = 2
C1, C3, C5 = 3.4445, -4.775, 2.0315
EPS = 1e-07
MESH = pl.DeviceIdType.MESH
VMEM_LIMIT = 66_000_000
PAIR = 2
COUNT = 3
LANES = 128
ROUNDS = 3
GROUPS = 4


def rounded(value):
    return value.astype(jnp.bfloat16)


def product(left, right):
    return jnp.dot(left, right, preferred_element_type=jnp.float32)


def token_sum(left, right):
    return lax.dot_general(
        left, right, (((0,), (0,)), ((), ())), preferred_element_type=jnp.float32
    )


def times_transpose(left, right):
    return lax.dot_general(
        left, right, (((1,), (1,)), ((), ())), preferred_element_type=jnp.float32
    )


def sigmoid_slope(pre_act):
    sigma = jax.nn.sigmoid(pre_act)
    return sigma, pre_act * sigma, sigma * (1.0 + pre_act * (1.0 - sigma))


def split(value):
    high = rounded(value)
    return (high, rounded(value - high.astype(jnp.float32)))


def dot_split(left, right, dot):
    along = 1 if dot is times_transpose else 0
    return dot(
        jnp.concatenate([left[0], left[0], left[1]], axis=1),
        jnp.concatenate([right[0], right[1], right[0]], axis=along),
    )


def place():
    me = lax.axis_index("seq")
    return me // PAIR, me % PAIR


def remote(src, dst, send, recv, device):
    copy = pltpu.make_async_remote_copy(
        src_ref=src,
        dst_ref=dst,
        send_sem=send,
        recv_sem=recv,
        device_id={"seq": device},
        device_id_type=MESH,
    )
    copy.start()
    return copy


def line_peer(lines, d):
    line, side = place()
    return lax.rem(line + d, lines) * PAIR + side


def partner():
    line, side = place()
    return line * PAIR + (1 - side)


def greet(lines):
    barrier = pltpu.get_barrier_semaphore()
    for peer in [partner()] + [line_peer(lines, d) for d in range(1, lines)]:
        pl.semaphore_signal(barrier, inc=1, device_id={"seq": peer}, device_id_type=MESH)


def greeted(lines):
    pl.semaphore_wait(pltpu.get_barrier_semaphore(), lines)


class Scatter:
    def __init__(self, lines, part, paired, middle, lined, sems):
        self.lines = lines
        self.part, self.paired, self.middle, self.lined = part, paired, middle, lined
        self.sems = sems

    def fill(self, total, at=0):
        n, rows, wide = self.part.shape
        for j in range(n):
            self.part[j] = rounded(total[j * rows : (j + 1) * rows, at : at + wide])

    def start(self):
        lines = self.lines
        line, side = place()
        self.pairs = {}
        for d in list(range(1, lines)) + [0]:
            to = lax.rem(line + d, lines)
            self.pairs[d] = remote(
                self.part.at[to * PAIR + (1 - side)],
                self.paired.at[d],
                self.sems.at[0, d],
                self.sems.at[1, d],
                partner(),
            )

    def forward(self):
        lines = self.lines
        line, side = place()
        self.sent = []
        for d in range(1, lines):
            to = lax.rem(line + d, lines)
            self.pairs[d].wait()
            self.middle[d] = rounded(
                self.part[to * PAIR + side].astype(jnp.float32)
                + self.paired[d].astype(jnp.float32)
            )
            self.sent.append(
                remote(
                    self.middle.at[d],
                    self.lined.at[d],
                    self.sems.at[2, d],
                    self.sems.at[3, d],
                    to * PAIR + side,
                )
            )

    def total(self):
        self.pairs[0].wait()
        me = lax.axis_index("seq")
        total = self.part[me].astype(jnp.float32) + self.paired[0].astype(jnp.float32)
        for d, copy in zip(range(1, self.lines), self.sent):
            copy.wait()
            total = total + self.lined[d].astype(jnp.float32)
        return total


class Reduce(Scatter):
    def __init__(self, lines, part, paired, middle, lined, sems, mine, gathered, crossed):
        super().__init__(lines, part, paired, middle, lined, sems)
        self.mine, self.gathered, self.crossed = mine, gathered, crossed

    def gather(self):
        self.mine[...] = rounded(self.total())
        self.out = []
        for d in range(1, self.lines):
            self.out.append(
                remote(
                    self.mine,
                    self.gathered.at[d],
                    self.sems.at[4, d],
                    self.sems.at[5, d],
                    line_peer(self.lines, d),
                )
            )
        self.across = [
            remote(
                self.mine, self.crossed.at[0], self.sems.at[6, 0], self.sems.at[7, 0], partner()
            )
        ]

    def relay(self):
        for d in range(1, self.lines):
            self.out[d - 1].wait()
            self.across.append(
                remote(
                    self.gathered.at[d],
                    self.crossed.at[d],
                    self.sems.at[6, d],
                    self.sems.at[7, d],
                    partner(),
                )
            )

    def finish(self, put):
        lines = self.lines
        line, side = place()
        rows = self.mine.shape[0]

        def place_block(owner, block):
            put(pl.ds(pl.multiple_of(owner * rows, rows), rows), block.astype(jnp.float32))

        place_block(line * PAIR + side, self.mine[...])
        for d in range(1, lines):
            place_block(lax.rem(line - d + lines, lines) * PAIR + side, self.gathered[d])
        for d in range(lines):
            self.across[d].wait()
            place_block(lax.rem(line - d + lines, lines) * PAIR + (1 - side), self.crossed[d])


def ns_forward(s, m):
    matrix = s.totals[m]
    norm = jnp.sqrt(jnp.sum(matrix * matrix))
    s.current[m] = matrix / (norm + EPS)

    def keep(k, x, gram, poly):
        s.xs[k, m], s.grams[k, m], s.polys[k, m] = x, gram, poly

    def single(k, carry):
        x = rounded(s.current[m])
        gram = times_transpose(x, x)
        gram_r = rounded(gram)
        poly = rounded(C3 * gram + C5 * product(gram_r, gram_r))
        keep(k, x, gram_r, poly)
        s.current[m] = C1 * s.current[m] + product(poly, x)
        return carry

    def precise(k, carry):
        xp = split(s.current[m])
        gram = dot_split(xp, xp, times_transpose)
        gp = split(gram)
        poly = split(C3 * gram + C5 * dot_split(gp, gp, product))
        keep(k, xp[0], gp[0], poly[0])
        s.current[m] = C1 * s.current[m] + dot_split(poly, xp, product)
        return carry

    lax.fori_loop(0, NS_SINGLE, single, 0)
    lax.fori_loop(NS_SINGLE, NS_STEPS, precise, 0)


def ns_backward(s, m):
    s.current[m] = s.adjoint[m]

    def step(i, carry):
        k = NS_STEPS - 1 - i
        grad = s.current[m]
        grad_r, x = rounded(grad), s.xs[k, m]
        dpoly = times_transpose(grad_r, x)
        sym = dpoly + dpoly.T
        twist = product(rounded(sym), s.grams[k, m])
        weight = rounded(C3 * sym + C5 * (twist + twist.T))
        s.current[m] = C1 * grad + product(
            jnp.concatenate([s.polys[k, m], weight], axis=1),
            jnp.concatenate([grad_r, x], axis=0),
        )
        return carry

    lax.fori_loop(0, NS_STEPS, step, 0)
    matrix, grad = s.totals[m], s.current[m]
    norm = jnp.sqrt(jnp.sum(matrix * matrix))
    shifted = norm + EPS
    dot_all = jnp.sum(grad * matrix)
    return grad / shifted - matrix * (dot_all / (norm * shifted * shifted))


OPERANDS = (
    "inputs", "rates", "proj_query", "proj_key", "proj_value", "proj_output",
    "fast_in", "fast_up", "fast_out", "cotangent",
)
RESULTS = (
    "grads_hbm", "rate_hbm", "in_hbm", "up_hbm", "out_hbm",
    "query_hbm", "key_hbm", "value_hbm", "output_hbm",
)


def scratch_of(n, tokens, width, h, f):
    lines = n // PAIR
    rows, wide_rows = h // n, width // n
    bf16, f32 = jnp.bfloat16, jnp.float32
    tile = math.gcd(tokens, 256)
    v = pltpu.VMEM
    return dict(
        x=v((tokens, width), bf16),
        cot=v((tokens, width), bf16),
        x_t=v((width, tokens), bf16),
        cot_t=v((width, tokens), bf16),
        wall=v((width, 3 * h), bf16),
        wo=v((h, width), bf16),
        rates_in=v((tokens // LANES, LANES), f32),
        rate_cols=v((tokens, LANES), f32),
        fin=v((h, f), f32),
        fup=v((h, f), f32),
        fout=v((f, h), f32),
        fout_t=v((h, f), f32),
        b4=v((h, 4 * f), bf16),
        bow=v((h, 2 * f), bf16),
        nw=v((h, 2 * f), bf16),
        no_t=v((h, f), bf16),
        key=v((tokens, h), bf16),
        value=v((tokens, h), bf16),
        scaled=v((tokens, h), bf16),
        key_t=v((h, tokens), bf16),
        scaled_t=v((h, tokens), bf16),
        query=v((tokens, h), bf16),
        back_out=v((tokens, h), bf16),
        pre=v((tokens, 2 * f), f32),
        ups=v((tokens, f), f32),
        work=v((tile, 3 * f), f32),
        hb=v((tokens, 2 * f), bf16),
        g4=v((tokens, 4 * f), bf16),
        hq=v((tokens, f), bf16),
        bpr=v((tokens, 2 * f), bf16),
        grads=v((tokens, 3 * h), bf16),
        orow=v((tokens, h), bf16),
        rate_out=v((tokens // LANES, LANES), f32),
        xs=v((NS_STEPS, COUNT, h, f), bf16),
        grams=v((NS_STEPS, COUNT, h, h), bf16),
        polys=v((NS_STEPS, COUNT, h, h), bf16),
        current=v((COUNT, h, f), f32),
        totals=v((COUNT, h, f), f32),
        adjoint=v((COUNT, h, f), f32),
        gout=v((f, h), f32),
        row_sums=v((GROUPS - 1, wide_rows, h), f32),
        output_sum=v((h, wide_rows), f32),
        part=v((COUNT, n, rows, f), bf16),
        middle=v((COUNT, lines, rows, f), bf16),
        mine=v((COUNT, rows, f), bf16),
        paired=v((ROUNDS, COUNT, lines, rows, f), bf16),
        lined=v((ROUNDS, COUNT, lines, rows, f), bf16),
        gathered=v((ROUNDS, COUNT, lines, rows, f), bf16),
        crossed=v((ROUNDS, COUNT, lines, rows, f), bf16),
        sems=pltpu.SemaphoreType.DMA((ROUNDS, COUNT, 8, lines)),
        row_part=v((GROUPS, n, wide_rows, h), bf16),
        row_paired=v((GROUPS, lines, wide_rows, h), bf16),
        row_middle=v((GROUPS, lines, wide_rows, h), bf16),
        row_lined=v((GROUPS, lines, wide_rows, h), bf16),
        row_sems=pltpu.SemaphoreType.DMA((GROUPS, 4, lines)),
        load_sems=pltpu.SemaphoreType.DMA((8,)),
        x_sems=pltpu.SemaphoreType.DMA((tokens // tile,)),
        cot_sems=pltpu.SemaphoreType.DMA((tokens // tile,)),
        store_sems=pltpu.SemaphoreType.DMA((len(RESULTS),)),
    )


def kernel(n, names, *refs):
    s = SimpleNamespace(**dict(zip(names, refs)))
    lines = n // PAIR
    tokens, width = s.x.shape
    h, f = s.fin.shape
    tile = math.gcd(tokens, 256)
    tiles = tokens // tile
    sub = math.gcd(tile, 32)
    half = math.gcd(f, 256)
    f32 = jnp.float32

    def rows_at(i, size=tile):
        return pl.ds(pl.multiple_of(i * size, size), size)

    def over_tiles(step, first=0, last=tiles):
        def body(i, carry):
            step(i, rows_at(i))
            return carry

        lax.fori_loop(first, last, body, 0)

    def over_subs(step):
        def body(i, carry):
            for j in range(f // half):
                step(i, j * half)
            return carry

        lax.fori_loop(0, tile // sub, body, 0)

    def load(src, dst, sem):
        copy = pltpu.make_async_copy(src, dst, sem)
        copy.start()
        return copy

    def x_copy(i, at):
        return pltpu.make_async_copy(s.inputs.at[at], s.x.at[at], s.x_sems.at[i])

    def cot_copy(i, at):
        return pltpu.make_async_copy(s.cotangent.at[at], s.cot.at[at], s.cot_sems.at[i])

    reduces = [
        [
            Reduce(
                lines, s.part.at[c], s.paired.at[r, c], s.middle.at[c], s.lined.at[r, c],
                s.sems.at[r, c], s.mine.at[c], s.gathered.at[r, c], s.crossed.at[r, c],
            )
            for c in range(COUNT)
        ]
        for r in range(ROUNDS)
    ]
    scatters = [
        Scatter(
            lines, s.row_part.at[g], s.row_paired.at[g], s.row_middle.at[g], s.row_lined.at[g],
            s.row_sems.at[g],
        )
        for g in range(GROUPS)
    ]

    greet(lines)
    x_copy(0, pl.ds(0, tile)).start()
    loads = [
        load(s.proj_key, s.wall.at[:, h : 2 * h], s.load_sems.at[0]),
        load(s.proj_value, s.wall.at[:, 2 * h :], s.load_sems.at[1]),
        load(s.rates, s.rates_in, s.load_sems.at[2]),
        load(s.fast_in, s.fin, s.load_sems.at[3]),
        load(s.fast_up, s.fup, s.load_sems.at[4]),
        load(s.fast_out, s.fout, s.load_sems.at[5]),
    ]
    for i in range(1, tiles):
        x_copy(i, pl.ds(i * tile, tile)).start()
    loads += [
        load(s.proj_query, s.wall.at[:, :h], s.load_sems.at[6]),
        load(s.proj_output, s.wo, s.load_sems.at[7]),
    ]
    for i in range(tiles):
        cot_copy(i, pl.ds(i * tile, tile)).start()

    for copy in loads[:6]:
        copy.wait()
    s.b4[:, 2 * f : 3 * f] = rounded(s.fin[...])
    s.b4[:, 3 * f :] = rounded(s.fup[...])
    s.fout_t[...] = s.fout[...].T
    s.bow[:, f:] = rounded(s.fout_t[...])
    for i in range(tokens // LANES):
        s.rate_cols[i * LANES : (i + 1) * LANES, :] = jnp.broadcast_to(
            s.rates_in[i : i + 1, :], (LANES, LANES)
        ).T

    def rate_of(at, wide):
        return jnp.concatenate([s.rate_cols[at, :]] * (wide // LANES), axis=1)

    def update(i, at):
        x_copy(i, at).wait()
        both = product(s.x[at, :], s.wall[:, h:])
        key = rounded(both[:, :h])
        value = rounded(both[:, h:])
        scaled = rounded(rate_of(at, h) * value.astype(f32))
        s.key[at, :], s.value[at, :], s.scaled[at, :] = key, value, scaled
        s.pre[at, :] = product(key, s.b4[:, 2 * f :])
        s.ups[at, :] = product(scaled, s.bow[:, f:])
        s.key_t[:, at] = key.T
        s.scaled_t[:, at] = scaled.T

        def point(j, col):
            to = pl.ds(pl.multiple_of(i * tile + j * sub, sub), sub)
            pre_in, pre_up = s.pre[to, col : col + half], s.pre[to, f + col : f + col + half]
            up = s.ups[to, col : col + half]
            _, activation, slope = sigmoid_slope(pre_in)
            s.hb[to, col : col + half] = rounded(activation * pre_up)
            s.g4[to, col : col + half] = rounded(up * pre_up * slope)
            s.g4[to, f + col : f + col + half] = rounded(up * activation)

        over_subs(point)

    over_tiles(update)
    greeted(lines)
    now = reduces[0]
    now[0].fill(product(s.key_t[...], s.g4[:, :f]))
    now[0].start()
    now[1].fill(product(s.key_t[...], s.g4[:, f : 2 * f]))
    now[1].start()
    now[2].fill(product(s.scaled_t[...], s.hb[:, :f]))
    now[2].start()

    def total_put(m):
        def put(at, block):
            s.totals[m, at, :] = block

        return put

    def project(i, at):
        s.query[at, :] = rounded(product(s.x[at, :], s.wall[:, :h]))
        cot_copy(i, at).wait()
        s.back_out[at, :] = rounded(times_transpose(s.cot[at, :], s.wo[...]))

    def turn(i, at):
        s.x_t[:, at] = s.x[at, :].T
        s.cot_t[:, at] = s.cot[at, :].T

    for copy in loads[6:]:
        copy.wait()
    now[0].forward()
    over_tiles(project)
    now[1].forward()
    now[0].gather()
    over_tiles(turn)
    now[2].forward()
    now[1].gather()
    now[0].relay()
    now[2].gather()
    now[0].finish(total_put(0))
    now[1].relay()
    ns_forward(s, 0)
    now[2].relay()
    now[1].finish(total_put(1))
    ns_forward(s, 1)
    s.nw[:, :f] = rounded(s.fin[...] + s.current[0])
    s.nw[:, f:] = rounded(s.fup[...] + s.current[1])
    now[2].finish(total_put(2))
    ns_forward(s, 2)
    s.no_t[...] = rounded(s.fout_t[...] + s.current[2])

    def query(i, at):
        s.work[:, : 2 * f] = product(s.query[at, :], s.nw[...])
        s.work[:, 2 * f :] = product(s.back_out[at, :], s.no_t[...])

        def point(j, col):
            here = rows_at(j, sub)
            to = pl.ds(pl.multiple_of(i * tile + j * sub, sub), sub)
            pre_p = s.work[here, col : col + half]
            pre_r = s.work[here, f + col : f + col + half]
            back = s.work[here, 2 * f + col : 2 * f + col + half]
            _, activation, slope = sigmoid_slope(pre_p)
            s.hq[to, col : col + half] = rounded(activation * pre_r)
            s.bpr[to, col : col + half] = rounded(back * pre_r * slope)
            s.bpr[to, f + col : f + col + half] = rounded(back * activation)

        over_subs(point)

    over_tiles(query)
    now = reduces[1]
    now[2].fill(token_sum(s.back_out[...], s.hq[...]))
    now[2].start()
    query_sums = token_sum(s.query[...], s.bpr[...])
    now[0].fill(query_sums)
    now[0].start()
    now[1].fill(query_sums, f)
    now[1].start()

    def adjoint_put(m):
        def put(at, block):
            s.adjoint[m, at, :] = block

        return put

    def query_back(i, at):
        s.grads[at, :h] = rounded(times_transpose(s.bpr[at, :], s.nw[...]))
        s.orow[at, :] = rounded(times_transpose(s.hq[at, :], s.no_t[...]))

    now[2].forward()
    over_tiles(query_back)
    now[0].forward()
    now[2].gather()
    scatters[0].fill(product(s.x_t[...], s.grads[:, :h]))
    now[1].forward()
    now[0].gather()
    now[2].relay()
    scatters[1].fill(product(s.cot_t[...], s.orow[...]))
    now[1].gather()
    now[2].finish(adjoint_put(2))
    now[0].relay()
    s.bow[:, :f] = rounded(ns_backward(s, 2))
    now[1].relay()
    scatters[0].start()
    now[0].finish(adjoint_put(0))
    s.b4[:, :f] = rounded(ns_backward(s, 0))
    scatters[1].start()
    now[1].finish(adjoint_put(1))
    s.b4[:, f : 2 * f] = rounded(ns_backward(s, 1))
    scatters[0].forward()

    def update_back(i, at):
        s.work[:, : 2 * f] = product(s.key[at, :], s.b4[:, : 2 * f])
        s.work[:, 2 * f :] = product(s.scaled[at, :], s.bow[:, :f])

        def point(j, col):
            here = rows_at(j, sub)
            to = pl.ds(pl.multiple_of(i * tile + j * sub, sub), sub)
            press_in = s.work[here, col : col + half]
            press_up = s.work[here, f + col : f + col + half]
            back_hid = s.work[here, 2 * f + col : 2 * f + col + half]
            pre_in, pre_up = s.pre[to, col : col + half], s.pre[to, f + col : f + col + half]
            up = s.ups[to, col : col + half]
            sigma, activation, slope = sigmoid_slope(pre_in)
            rest = 1.0 - sigma
            curvature = sigma * rest * (2.0 + pre_in * (rest - sigma))
            press_slope = press_in * slope
            s.hb[to, f + col : f + col + half] = rounded(press_slope * pre_up + press_up * activation)
            s.g4[to, 3 * f + col : 3 * f + col + half] = rounded(
                press_slope * up + back_hid * activation
            )
            s.g4[to, 2 * f + col : 2 * f + col + half] = rounded(
                press_in * up * pre_up * curvature + (press_up * up + back_hid * pre_up) * slope
            )

        over_subs(point)

    over_tiles(update_back)
    now = reduces[2]
    now[2].fill(product(s.scaled_t[...], s.hb[:, f:]))
    now[2].start()
    now[0].fill(product(s.key_t[...], s.g4[:, 2 * f : 3 * f]))
    now[0].start()
    now[1].fill(product(s.key_t[...], s.g4[:, 3 * f :]))
    now[1].start()
    scatters[1].forward()

    def token_back(i, at):
        back_scaled = times_transpose(s.hb[at, :], s.bow[...])
        weighed = back_scaled * s.value[at, :].astype(f32)
        for t in range(tile // LANES):
            block = weighed[t * LANES : (t + 1) * LANES, :]
            folded = block[:, :LANES]
            for c in range(1, h // LANES):
                folded = folded + block[:, c * LANES : (c + 1) * LANES]
            s.rate_out[pl.ds(i * (tile // LANES) + t, 1), :] = jnp.sum(
                folded.T, axis=0, keepdims=True
            )
        s.grads[at, 2 * h :] = rounded(rate_of(at, h) * back_scaled)
        s.grads[at, h : 2 * h] = rounded(times_transpose(s.g4[at, :], s.b4[...]))

    over_tiles(token_back, 0, tiles // 2)
    now[2].forward()
    over_tiles(token_back, tiles // 2, tiles)
    stores = [
        load(s.grads, s.grads_hbm, s.store_sems.at[0]),
        load(s.rate_out, s.rate_hbm, s.store_sems.at[1]),
    ]
    now[0].forward()
    now[2].gather()
    key_value = product(s.x_t[...], s.grads[:, h:])
    scatters[2].fill(key_value)
    scatters[2].start()
    scatters[3].fill(key_value, h)
    scatters[3].start()
    now[1].forward()
    now[0].gather()
    now[2].relay()
    now[1].gather()
    now[0].relay()
    scatters[2].forward()
    now[1].relay()
    scatters[3].forward()

    def sum_put(m):
        def put(at, block):
            s.totals[m, at, :] = s.adjoint[m, at, :] + block

        return put

    s.row_sums[0] = scatters[0].total()
    stores.append(load(s.row_sums.at[0], s.query_hbm, s.store_sems.at[5]))
    s.output_sum[...] = scatters[1].total().T
    stores.append(load(s.output_sum, s.output_hbm, s.store_sems.at[8]))
    now[2].finish(sum_put(2))
    s.gout[...] = s.totals[2].T
    stores.append(load(s.gout, s.out_hbm, s.store_sems.at[4]))
    now[0].finish(sum_put(0))
    stores.append(load(s.totals.at[0], s.in_hbm, s.store_sems.at[2]))
    s.row_sums[1] = scatters[2].total()
    stores.append(load(s.row_sums.at[1], s.key_hbm, s.store_sems.at[6]))
    s.row_sums[2] = scatters[3].total()
    stores.append(load(s.row_sums.at[2], s.value_hbm, s.store_sems.at[7]))
    now[1].finish(sum_put(1))
    stores.append(load(s.totals.at[1], s.up_hbm, s.store_sems.at[3]))
    for copy in stores:
        copy.wait()


def last_kernel(grads, proj_query, proj_key, proj_value, *rest):
    back_inputs, copies = rest[len(rest) // 2], rest[: len(rest) // 2]
    weights = jnp.concatenate([proj_query[...], proj_key[...], proj_value[...]], axis=1)
    back_inputs[...] = rounded(times_transpose(grads[...], weights))
    for src, dst in zip(copies, rest[len(rest) // 2 + 1 :]):
        dst[...] = src[...]


def body(n, *operands):
    inputs, rates, fast_in = operands[0], operands[1], operands[6]
    tokens, width = inputs.shape
    h, f = fast_in.shape
    wide_rows = width // n
    bf16, f32 = jnp.bfloat16, jnp.float32
    outs = [
        ((tokens, 3 * h), bf16),
        ((tokens // LANES, LANES), f32),
        ((h, f), f32),
        ((h, f), f32),
        ((f, h), f32),
        ((wide_rows, h), f32),
        ((wide_rows, h), f32),
        ((wide_rows, h), f32),
        ((h, wide_rows), f32),
    ]
    scratch = scratch_of(n, tokens, width, h, f)
    anywhere = pl.BlockSpec(memory_space=pl.ANY)
    operands = list(operands)
    operands[1] = rates.reshape(tokens // LANES, LANES)
    results = pl.pallas_call(
        functools.partial(kernel, n, OPERANDS + RESULTS + tuple(scratch)),
        out_shape=[jax.ShapeDtypeStruct(shape, kind) for shape, kind in outs],
        in_specs=[anywhere] * len(operands),
        out_specs=[anywhere] * len(outs),
        scratch_shapes=list(scratch.values()),
        compiler_params=pltpu.CompilerParams(
            collective_id=0, has_side_effects=True, vmem_limit_bytes=VMEM_LIMIT
        ),
    )(*operands)

    grads, rest = results[0], results[1:]
    tile = math.gcd(tokens, 256)
    whole = lambda array: pl.BlockSpec(array.shape, lambda i: (0,) * array.ndim)
    token_block = pl.BlockSpec((tile, width), lambda i: (i, 0))
    return pl.pallas_call(
        lambda *refs: last_kernel(*refs),
        grid=(tokens // tile,),
        out_shape=[jax.ShapeDtypeStruct((tokens, width), bf16)]
        + [jax.ShapeDtypeStruct(r.shape, r.dtype) for r in rest],
        in_specs=[pl.BlockSpec((tile, 3 * h), lambda i: (i, 0))]
        + [whole(w) for w in operands[2:5]]
        + [whole(r) for r in rest],
        out_specs=[token_block] + [whole(r) for r in rest],
    )(grads, *operands[2:5], *rest)


def solution(mesh):
    n = mesh.shape["seq"]

    def step(*operands):
        outs = body(n, *operands)
        return (outs[0], outs[1].reshape(-1)) + tuple(outs[2:])

    in_specs = (
        P(("batch", "seq"), None),
        P(("batch", "seq")),
        P(),
        P(),
        P(),
        P(),
        P(),
        P(),
        P(),
        P(("batch", "seq"), None),
    )
    out_specs = (
        P(("batch", "seq"), None),
        P(("batch", "seq")),
        P("batch", None),
        P("batch", None),
        P("batch", None),
        P("seq", "batch"),
        P("seq", "batch"),
        P("seq", "batch"),
        P("batch", "seq"),
    )
    return jax.shard_map(
        step, mesh=mesh, in_specs=in_specs, out_specs=out_specs, check_vma=False
    )
```

time: 174 us -> 131 us (0.75)
  matrix products: 27.1 us -> 0 us
  local copies, waits for them, and re-layouts: 10.9 us -> 1.64 us
  Pallas kernels: 132 us -> 129 us
  other arithmetic: 2.79 us -> 0 us
    dot_general x29 -> x0, matrix products: 27.1 us -> none  [the longest x11 12.2 us: product(): return jnp.dot(left, right, preferred_element_type=jnp.float32)]
    unnamed x66 -> x1, local copies, waits for them, and re-layouts: 10.2 us -> 1.64 us
    pallas_call x3 -> x2, Pallas kernels: 132 us -> 129 us  [the longest x1 123 us: body(): pl.pallas_call(functools.partial(kernel, n, OPERANDS + RESULTS + tuple(sc...]
    concatenate x3 -> x0, other arithmetic: 2.79 us -> none  [stacked(): return jnp.concatenate([rounded(t) for t in terms]).reshape((n,) + block)]
where the time goes in v1:
time: 131 us
  Pallas kernels  129 us (98%)
  local copies, waits for them, and re-layouts  1.64 us (1%)
    pallas_call x1, Pallas kernels, body(): pl.pallas_call(functools.partial(kernel, n, OPERANDS + RESULTS + tuple(sc...  123 us
    pallas_call x1, Pallas kernels, body(): pl.pallas_call(lambda *refs: last_kernel(*refs), grid=(tokens // tile,),...  6.14 us

profile of v1, /device:TPU:0, one launch (start us, length us, event | category | flops | bytes accessed | tf_op | source)
XLA Modules:
  0.0 131.1 jit_solution(11543094912282534028)
XLA Ops:
  0.6 122.7 %shard_map.169 = (bf16[1024,768]{1,0:T(8,128)(2,1)}, f32[8,128]{1,0:T(8,128)}, f32[256,512]{1,0:T(8,128)}, f32[256,512]{1,0:T(8,128)}, f32[512,256]{1,0:T(8,128)...) custom-call(bf16[1024,768]{1,0:T(8,128)(2,1)} %refs_0_.1, f32[8,128]{1,0:T(8,128)} %bitcast.2, ...), custom_call_target="tpu_custom_call" | custom-call | tf_op jit(solution)/shard_map/pallas_call | solution.py:692
  123.3 6.1 %shard_map.170 = (bf16[1024,768]{1,0:T(8,128)(2,1)}, f32[8,128]{1,0:T(8,128)}, f32[256,512]{1,0:T(8,128)}, f32[256,512]{1,0:T(8,128)}, f32[512,256]{1,0:T(8,128)...) custom-call(bf16[1024,768]{1,0:T(8,128)(2,1)} %get-tuple-element.27.refs_0_, ...), custom_call_target="tpu_custom_call" | custom-call | tf_op jit(solution)/shard_map/pallas_call | solution.py:707
  129.5 1.6 %copy.19 = f32[256,96]{0,1:T(8,128)} copy(f32[256,96]{1,0:T(8,128)} %get-tuple-element.53) | data formatting | bytes 196608

commit v2 on v1

--- a/solution.py
+++ b/solution.py
@@ -20,6 +20,7 @@
 LANES = 128
 ROUNDS = 3
 GROUPS = 4
+PIECE = 384 * 1024
 
 
 def rounded(value):
@@ -50,14 +51,6 @@
 def split(value):
     high = rounded(value)
     return (high, rounded(value - high.astype(jnp.float32)))
-
-
-def dot_split(left, right, dot):
-    along = 1 if dot is times_transpose else 0
-    return dot(
-        jnp.concatenate([left[0], left[0], left[1]], axis=1),
-        jnp.concatenate([right[0], right[1], right[0]], axis=along),
-    )
 
 
 def place():
@@ -207,59 +200,82 @@
             place_block(lax.rem(line - d + lines, lines) * PAIR + (1 - side), self.crossed[d])
 
 
-def ns_forward(s, m):
-    matrix = s.totals[m]
-    norm = jnp.sqrt(jnp.sum(matrix * matrix))
-    s.current[m] = matrix / (norm + EPS)
-
-    def keep(k, x, gram, poly):
+def squared(parts, dot):
+    along = 0 if dot is times_transpose else 1
+    both = dot(parts[0], jnp.concatenate(parts, axis=along))
+    wide = both.shape[1] // 2
+    return both[:, :wide] + (both[:, wide:] + both[:, wide:].T)
+
+
+def ns_forward(s):
+    each = range(COUNT)
+    for m in each:
+        matrix = s.totals[m]
+        s.current[m] = matrix / (jnp.sqrt(jnp.sum(matrix * matrix)) + EPS)
+
+    def keep(k, m, x, gram, poly):
         s.xs[k, m], s.grams[k, m], s.polys[k, m] = x, gram, poly
 
     def single(k, carry):
-        x = rounded(s.current[m])
-        gram = times_transpose(x, x)
-        gram_r = rounded(gram)
-        poly = rounded(C3 * gram + C5 * product(gram_r, gram_r))
-        keep(k, x, gram_r, poly)
-        s.current[m] = C1 * s.current[m] + product(poly, x)
+        xs = [rounded(s.current[m]) for m in each]
+        grams = [times_transpose(x, x) for x in xs]
+        grams_r = [rounded(gram) for gram in grams]
+        polys = [rounded(C3 * g + C5 * product(r, r)) for g, r in zip(grams, grams_r)]
+        for m in each:
+            keep(k, m, xs[m], grams_r[m], polys[m])
+            s.current[m] = C1 * s.current[m] + product(polys[m], xs[m])
         return carry
 
     def precise(k, carry):
-        xp = split(s.current[m])
-        gram = dot_split(xp, xp, times_transpose)
-        gp = split(gram)
-        poly = split(C3 * gram + C5 * dot_split(gp, gp, product))
-        keep(k, xp[0], gp[0], poly[0])
-        s.current[m] = C1 * s.current[m] + dot_split(poly, xp, product)
+        xs = [split(s.current[m]) for m in each]
+        grams = [squared(x, times_transpose) for x in xs]
+        parts = [split(gram) for gram in grams]
+        polys = [split(C3 * g + C5 * squared(p, product)) for g, p in zip(grams, parts)]
+        for m in each:
+            keep(k, m, xs[m][0], parts[m][0], polys[m][0])
+            tall = product(jnp.concatenate(polys[m], axis=0), xs[m][0])
+            rows = tall.shape[0] // 2
+            s.current[m] = (
+                C1 * s.current[m]
+                + (tall[:rows] + tall[rows:])
+                + product(polys[m][0], xs[m][1])
+            )
         return carry
 
     lax.fori_loop(0, NS_SINGLE, single, 0)
     lax.fori_loop(NS_SINGLE, NS_STEPS, precise, 0)
 
 
-def ns_backward(s, m):
-    s.current[m] = s.adjoint[m]
+def ns_backward(s):
+    each = range(COUNT)
+    for m in each:
+        s.current[m] = s.adjoint[m]
 
     def step(i, carry):
         k = NS_STEPS - 1 - i
-        grad = s.current[m]
-        grad_r, x = rounded(grad), s.xs[k, m]
-        dpoly = times_transpose(grad_r, x)
-        sym = dpoly + dpoly.T
-        twist = product(rounded(sym), s.grams[k, m])
-        weight = rounded(C3 * sym + C5 * (twist + twist.T))
-        s.current[m] = C1 * grad + product(
-            jnp.concatenate([s.polys[k, m], weight], axis=1),
-            jnp.concatenate([grad_r, x], axis=0),
+        grads = [rounded(s.current[m]) for m in each]
+        dpolys = [times_transpose(grads[m], s.xs[k, m]) for m in each]
+        syms = [dpoly + dpoly.T for dpoly in dpolys]
+        twists = [product(rounded(syms[m]), s.grams[k, m]) for m in each]
+        weights = [rounded(C3 * sym + C5 * (t + t.T)) for sym, t in zip(syms, twists)]
+        for m in each:
+            s.current[m] = C1 * s.current[m] + product(
+                jnp.concatenate([s.polys[k, m], weights[m]], axis=1),
+                jnp.concatenate([grads[m], s.xs[k, m]], axis=0),
+            )
+        return carry
+
+    lax.fori_loop(0, NS_STEPS, step, 0)
+    results = []
+    for m in each:
+        matrix, grad = s.totals[m], s.current[m]
+        norm = jnp.sqrt(jnp.sum(matrix * matrix))
+        shifted = norm + EPS
+        dot_all = jnp.sum(grad * matrix)
+        results.append(
+            rounded(grad / shifted - matrix * (dot_all / (norm * shifted * shifted)))
         )
-        return carry
-
-    lax.fori_loop(0, NS_STEPS, step, 0)
-    matrix, grad = s.totals[m], s.current[m]
-    norm = jnp.sqrt(jnp.sum(matrix * matrix))
-    shifted = norm + EPS
-    dot_all = jnp.sum(grad * matrix)
-    return grad / shifted - matrix * (dot_all / (norm * shifted * shifted))
+    return results
 
 
 OPERANDS = (
@@ -267,7 +283,7 @@
     "fast_in", "fast_up", "fast_out", "cotangent",
 )
 RESULTS = (
-    "grads_hbm", "rate_hbm", "in_hbm", "up_hbm", "out_hbm",
+    "back_hbm", "rate_hbm", "in_hbm", "up_hbm", "out_hbm",
     "query_hbm", "key_hbm", "value_hbm", "output_hbm",
 )
 
@@ -319,8 +335,7 @@
         totals=v((COUNT, h, f), f32),
         adjoint=v((COUNT, h, f), f32),
         gout=v((f, h), f32),
-        row_sums=v((GROUPS - 1, wide_rows, h), f32),
-        output_sum=v((h, wide_rows), f32),
+        row_sums=v((GROUPS, wide_rows, h), f32),
         part=v((COUNT, n, rows, f), bf16),
         middle=v((COUNT, lines, rows, f), bf16),
         mine=v((COUNT, rows, f), bf16),
@@ -491,16 +506,13 @@
     now[1].gather()
     now[0].relay()
     now[2].gather()
-    now[0].finish(total_put(0))
     now[1].relay()
-    ns_forward(s, 0)
     now[2].relay()
-    now[1].finish(total_put(1))
-    ns_forward(s, 1)
+    for m in range(COUNT):
+        now[m].finish(total_put(m))
+    ns_forward(s)
     s.nw[:, :f] = rounded(s.fin[...] + s.current[0])
     s.nw[:, f:] = rounded(s.fup[...] + s.current[1])
-    now[2].finish(total_put(2))
-    ns_forward(s, 2)
     s.no_t[...] = rounded(s.fout_t[...] + s.current[2])
 
     def query(i, at):
@@ -550,16 +562,13 @@
     now[2].relay()
     scatters[1].fill(product(s.cot_t[...], s.orow[...]))
     now[1].gather()
-    now[2].finish(adjoint_put(2))
     now[0].relay()
-    s.bow[:, :f] = rounded(ns_backward(s, 2))
     now[1].relay()
     scatters[0].start()
-    now[0].finish(adjoint_put(0))
-    s.b4[:, :f] = rounded(ns_backward(s, 0))
     scatters[1].start()
-    now[1].finish(adjoint_put(1))
-    s.b4[:, f : 2 * f] = rounded(ns_backward(s, 1))
+    for m in (2, 0, 1):
+        now[m].finish(adjoint_put(m))
+    s.b4[:, :f], s.b4[:, f : 2 * f], s.bow[:, :f] = ns_backward(s)
     scatters[0].forward()
 
     def update_back(i, at):
@@ -616,7 +625,6 @@
     now[2].forward()
     over_tiles(token_back, tiles // 2, tiles)
     stores = [
-        load(s.grads, s.grads_hbm, s.store_sems.at[0]),
         load(s.rate_out, s.rate_hbm, s.store_sems.at[1]),
     ]
     now[0].forward()
@@ -628,6 +636,12 @@
     scatters[3].start()
     now[1].forward()
     now[0].gather()
+
+    def inputs_back(i, at):
+        s.cot[at, :] = rounded(times_transpose(s.grads[at, :], s.wall[...]))
+
+    over_tiles(inputs_back)
+    stores.append(load(s.cot, s.back_hbm, s.store_sems.at[0]))
     now[2].relay()
     now[1].gather()
     now[0].relay()
@@ -641,31 +655,55 @@
 
         return put
 
-    s.row_sums[0] = scatters[0].total()
-    stores.append(load(s.row_sums.at[0], s.query_hbm, s.store_sems.at[5]))
-    s.output_sum[...] = scatters[1].total().T
-    stores.append(load(s.output_sum, s.output_hbm, s.store_sems.at[8]))
+    for g, (to, sem) in enumerate(((s.query_hbm, 5), (s.output_hbm, 8))):
+        s.row_sums[g] = scatters[g].total()
+        stores.append(load(s.row_sums.at[g], to, s.store_sems.at[sem]))
     now[2].finish(sum_put(2))
     s.gout[...] = s.totals[2].T
     stores.append(load(s.gout, s.out_hbm, s.store_sems.at[4]))
     now[0].finish(sum_put(0))
     stores.append(load(s.totals.at[0], s.in_hbm, s.store_sems.at[2]))
-    s.row_sums[1] = scatters[2].total()
-    stores.append(load(s.row_sums.at[1], s.key_hbm, s.store_sems.at[6]))
-    s.row_sums[2] = scatters[3].total()
-    stores.append(load(s.row_sums.at[2], s.value_hbm, s.store_sems.at[7]))
+    for g, (to, sem) in ((2, (s.key_hbm, 6)), (3, (s.value_hbm, 7))):
+        s.row_sums[g] = scatters[g].total()
+        stores.append(load(s.row_sums.at[g], to, s.store_sems.at[sem]))
     now[1].finish(sum_put(1))
     stores.append(load(s.totals.at[1], s.up_hbm, s.store_sems.at[3]))
     for copy in stores:
         copy.wait()
 
 
-def last_kernel(grads, proj_query, proj_key, proj_value, *rest):
-    back_inputs, copies = rest[len(rest) // 2], rest[: len(rest) // 2]
-    weights = jnp.concatenate([proj_query[...], proj_key[...], proj_value[...]], axis=1)
-    back_inputs[...] = rounded(times_transpose(grads[...], weights))
-    for src, dst in zip(copies, rest[len(rest) // 2 + 1 :]):
-        dst[...] = src[...]
+def pieces_of(shape, kind):
+    size = math.prod(shape) * jnp.dtype(kind).itemsize
+    count = max(1, min(size // PIECE, shape[0] // LANES))
+    while shape[0] % (16 * count) and count > 1:
+        count -= 1
+    step = shape[0] // count
+    return [pl.ds(i * step, step) for i in range(count)]
+
+
+def copy_kernel(count, *refs):
+    sources, targets, holds = (refs[i * count : (i + 1) * count] for i in range(3))
+    sems = refs[-1]
+    moves = [
+        (src.at[at], hold.at[at], dst.at[at])
+        for src, dst, hold in zip(sources, targets, holds)
+        for at in pieces_of(src.shape, src.dtype)
+    ]
+    loads = [
+        pltpu.make_async_copy(src, hold, sems.at[0, i])
+        for i, (src, hold, _) in enumerate(moves)
+    ]
+    stores = [
+        pltpu.make_async_copy(hold, dst, sems.at[1, i])
+        for i, (_, hold, dst) in enumerate(moves)
+    ]
+    for load in loads:
+        load.start()
+    for load, store in zip(loads, stores):
+        load.wait()
+        store.start()
+    for store in stores:
+        store.wait()
 
 
 def body(n, *operands):
@@ -675,7 +713,7 @@
     wide_rows = width // n
     bf16, f32 = jnp.bfloat16, jnp.float32
     outs = [
-        ((tokens, 3 * h), bf16),
+        ((tokens, width), bf16),
         ((tokens // LANES, LANES), f32),
         ((h, f), f32),
         ((h, f), f32),
@@ -683,7 +721,7 @@
         ((wide_rows, h), f32),
         ((wide_rows, h), f32),
         ((wide_rows, h), f32),
-        ((h, wide_rows), f32),
+        ((wide_rows, h), f32),
     ]
     scratch = scratch_of(n, tokens, width, h, f)
     anywhere = pl.BlockSpec(memory_space=pl.ANY)
@@ -700,20 +738,15 @@
         ),
     )(*operands)
 
-    grads, rest = results[0], results[1:]
-    tile = math.gcd(tokens, 256)
-    whole = lambda array: pl.BlockSpec(array.shape, lambda i: (0,) * array.ndim)
-    token_block = pl.BlockSpec((tile, width), lambda i: (i, 0))
+    moves = sum(len(pieces_of(shape, kind)) for shape, kind in outs)
     return pl.pallas_call(
-        lambda *refs: last_kernel(*refs),
-        grid=(tokens // tile,),
-        out_shape=[jax.ShapeDtypeStruct((tokens, width), bf16)]
-        + [jax.ShapeDtypeStruct(r.shape, r.dtype) for r in rest],
-        in_specs=[pl.BlockSpec((tile, 3 * h), lambda i: (i, 0))]
-        + [whole(w) for w in operands[2:5]]
-        + [whole(r) for r in rest],
-        out_specs=[token_block] + [whole(r) for r in rest],
-    )(grads, *operands[2:5], *rest)
+        functools.partial(copy_kernel, len(outs)),
+        out_shape=[jax.ShapeDtypeStruct(shape, kind) for shape, kind in outs],
+        in_specs=[anywhere] * len(outs),
+        out_specs=[anywhere] * len(outs),
+        scratch_shapes=[pltpu.VMEM(shape, kind) for shape, kind in outs]
+        + [pltpu.SemaphoreType.DMA((2, moves))],
+    )(*results)
 
 
 def solution(mesh):
@@ -721,7 +754,7 @@
 
     def step(*operands):
         outs = body(n, *operands)
-        return (outs[0], outs[1].reshape(-1)) + tuple(outs[2:])
+        return (outs[0], outs[1].reshape(-1)) + tuple(outs[2:8]) + (outs[8].T,)
 
     in_specs = (
         P(("batch", "seq"), None),

time: 131 us -> 118 us (0.901)
  Pallas kernels: 129 us -> 117 us
  local copies, waits for them, and re-layouts: 1.64 us -> 0 us
    pallas_call x1, Pallas kernels: 123 us -> 114 us  [body(): pl.pallas_call(functools.partial(kernel, n, OPERANDS + RESULTS + tuple(sc...]
    pallas_call x1, Pallas kernels: 6.14 us -> 3 us  [body(): pl.pallas_call(functools.partial(copy_kernel, len(outs)), out_shape=[jax....]
    unnamed x1 -> x0, local copies, waits for them, and re-layouts: 1.64 us -> none
where the time goes in v2:
time: 118 us
  Pallas kernels  117 us (99%)
    pallas_call x1, Pallas kernels, body(): pl.pallas_call(functools.partial(kernel, n, OPERANDS + RESULTS + tuple(sc...  114 us
    pallas_call x1, Pallas kernels, body(): pl.pallas_call(functools.partial(copy_kernel, len(outs)), out_shape=[jax....  3 us

profile of v2, /device:TPU:0, one launch (start us, length us, event | category | flops | bytes accessed | tf_op | source)
XLA Modules:
  0.0 117.8 jit_solution(7165872562122846026)
XLA Ops:
  0.6 114.0 %shard_map.169 = (bf16[1024,768]{1,0:T(8,128)(2,1)}, f32[8,128]{1,0:T(8,128)}, f32[256,512]{1,0:T(8,128)}, f32[256,512]{1,0:T(8,128)}, f32[512,256]{1,0:T(8,128)...) custom-call(bf16[1024,768]{1,0:T(8,128)(2,1)} %refs_0_.1, f32[8,128]{1,0:T(8,128)} %bitcast.3, ...), custom_call_target="tpu_custom_call" | custom-call | tf_op jit(solution)/shard_map/pallas_call | solution.py:730
  114.7 3.0 %shard_map.170 = (bf16[1024,768]{1,0:T(8,128)(2,1)}, f32[8,128]{1,0:T(8,128)}, f32[256,512]{1,0:T(8,128)}, f32[256,512]{1,0:T(8,128)}, f32[512,256]{1,0:T(8,128)...) custom-call(bf16[1024,768]{1,0:T(8,128)(2,1)} %get-tuple-element.27.refs_0_, ...), custom_call_target="tpu_custom_call" | custom-call | tf_op jit(solution)/shard_map/pallas_call | solution.py:742

commit v3 on v2

--- a/solution.py
+++ b/solution.py
@@ -246,10 +246,8 @@
     lax.fori_loop(NS_SINGLE, NS_STEPS, precise, 0)
 
 
-def ns_backward(s):
+def ns_backward(s, first, last):
     each = range(COUNT)
-    for m in each:
-        s.current[m] = s.adjoint[m]
 
     def step(i, carry):
         k = NS_STEPS - 1 - i
@@ -265,7 +263,11 @@
             )
         return carry
 
-    lax.fori_loop(0, NS_STEPS, step, 0)
+    lax.fori_loop(first, last, step, 0)
+
+
+def ns_finish(s):
+    each = range(COUNT)
     results = []
     for m in each:
         matrix, grad = s.totals[m], s.current[m]
@@ -305,7 +307,6 @@
         rate_cols=v((tokens, LANES), f32),
         fin=v((h, f), f32),
         fup=v((h, f), f32),
-        fout=v((f, h), f32),
         fout_t=v((h, f), f32),
         b4=v((h, 4 * f), bf16),
         bow=v((h, 2 * f), bf16),
@@ -325,15 +326,14 @@
         g4=v((tokens, 4 * f), bf16),
         hq=v((tokens, f), bf16),
         bpr=v((tokens, 2 * f), bf16),
-        grads=v((tokens, 3 * h), bf16),
-        orow=v((tokens, h), bf16),
+        **({} if 3 * h == width else dict(grads=v((tokens, 3 * h), bf16))),
         rate_out=v((tokens // LANES, LANES), f32),
         xs=v((NS_STEPS, COUNT, h, f), bf16),
         grams=v((NS_STEPS, COUNT, h, h), bf16),
         polys=v((NS_STEPS, COUNT, h, h), bf16),
         current=v((COUNT, h, f), f32),
         totals=v((COUNT, h, f), f32),
-        adjoint=v((COUNT, h, f), f32),
+        adjoint=v((COUNT, h, f), bf16),
         gout=v((f, h), f32),
         row_sums=v((GROUPS, wide_rows, h), f32),
         part=v((COUNT, n, rows, f), bf16),
@@ -361,6 +361,8 @@
     lines = n // PAIR
     tokens, width = s.x.shape
     h, f = s.fin.shape
+    if 3 * h == width:
+        s.grads = s.x
     tile = math.gcd(tokens, 256)
     tiles = tokens // tile
     sub = math.gcd(tile, 32)
@@ -370,6 +372,10 @@
     def rows_at(i, size=tile):
         return pl.ds(pl.multiple_of(i * size, size), size)
 
+    def each_tile(step, first=0, last=tiles):
+        for i in range(first, last):
+            step(i, pl.ds(i * tile, tile))
+
     def over_tiles(step, first=0, last=tiles):
         def body(i, carry):
             step(i, rows_at(i))
@@ -377,13 +383,14 @@
 
         lax.fori_loop(first, last, body, 0)
 
+    def rows_from(i, j):
+        start = i * tile + j * sub
+        return pl.ds(start if isinstance(start, int) else pl.multiple_of(start, sub), sub)
+
     def over_subs(step):
-        def body(i, carry):
+        for i in range(tile // sub):
             for j in range(f // half):
                 step(i, j * half)
-            return carry
-
-        lax.fori_loop(0, tile // sub, body, 0)
 
     def load(src, dst, sem):
         copy = pltpu.make_async_copy(src, dst, sem)
@@ -422,7 +429,7 @@
         load(s.rates, s.rates_in, s.load_sems.at[2]),
         load(s.fast_in, s.fin, s.load_sems.at[3]),
         load(s.fast_up, s.fup, s.load_sems.at[4]),
-        load(s.fast_out, s.fout, s.load_sems.at[5]),
+        load(s.fast_out, s.gout, s.load_sems.at[5]),
     ]
     for i in range(1, tiles):
         x_copy(i, pl.ds(i * tile, tile)).start()
@@ -437,7 +444,7 @@
         copy.wait()
     s.b4[:, 2 * f : 3 * f] = rounded(s.fin[...])
     s.b4[:, 3 * f :] = rounded(s.fup[...])
-    s.fout_t[...] = s.fout[...].T
+    s.fout_t[...] = s.gout[...].T
     s.bow[:, f:] = rounded(s.fout_t[...])
     for i in range(tokens // LANES):
         s.rate_cols[i * LANES : (i + 1) * LANES, :] = jnp.broadcast_to(
@@ -460,7 +467,7 @@
         s.scaled_t[:, at] = scaled.T
 
         def point(j, col):
-            to = pl.ds(pl.multiple_of(i * tile + j * sub, sub), sub)
+            to = rows_from(i, j)
             pre_in, pre_up = s.pre[to, col : col + half], s.pre[to, f + col : f + col + half]
             up = s.ups[to, col : col + half]
             _, activation, slope = sigmoid_slope(pre_in)
@@ -470,7 +477,27 @@
 
         over_subs(point)
 
-    over_tiles(update)
+    each_tile(update)
+    for copy in loads[6:]:
+        copy.wait()
+
+    def project(i, at):
+        s.query[at, :] = rounded(product(s.x[at, :], s.wall[:, :h]))
+        cot_copy(i, at).wait()
+        s.back_out[at, :] = rounded(times_transpose(s.cot[at, :], s.wo[...]))
+
+    def turn(i, at):
+        s.x_t[:, at] = s.x[at, :].T
+        s.cot_t[:, at] = s.cot[at, :].T
+
+    second = lax.rem(lax.axis_index("batch"), 2) == 0
+    first = jnp.logical_not(second)
+
+    @pl.when(second)
+    def _():
+        over_tiles(project)
+        over_tiles(turn)
+
     greeted(lines)
     now = reduces[0]
     now[0].fill(product(s.key_t[...], s.g4[:, :f]))
@@ -486,22 +513,23 @@
 
         return put
 
-    def project(i, at):
-        s.query[at, :] = rounded(product(s.x[at, :], s.wall[:, :h]))
-        cot_copy(i, at).wait()
-        s.back_out[at, :] = rounded(times_transpose(s.cot[at, :], s.wo[...]))
-
-    def turn(i, at):
-        s.x_t[:, at] = s.x[at, :].T
-        s.cot_t[:, at] = s.cot[at, :].T
-
-    for copy in loads[6:]:
-        copy.wait()
+    @pl.when(first)
+    def _():
+        over_tiles(project, 0, tiles // 2)
+
     now[0].forward()
-    over_tiles(project)
+
+    @pl.when(first)
+    def _():
+        over_tiles(project, tiles // 2, tiles)
+
     now[1].forward()
     now[0].gather()
-    over_tiles(turn)
+
+    @pl.when(first)
+    def _():
+        over_tiles(turn)
+
     now[2].forward()
     now[1].gather()
     now[0].relay()
@@ -520,8 +548,8 @@
         s.work[:, 2 * f :] = product(s.back_out[at, :], s.no_t[...])
 
         def point(j, col):
-            here = rows_at(j, sub)
-            to = pl.ds(pl.multiple_of(i * tile + j * sub, sub), sub)
+            here = pl.ds(j * sub, sub)
+            to = rows_from(i, j)
             pre_p = s.work[here, col : col + half]
             pre_r = s.work[here, f + col : f + col + half]
             back = s.work[here, 2 * f + col : 2 * f + col + half]
@@ -544,13 +572,13 @@
 
     def adjoint_put(m):
         def put(at, block):
-            s.adjoint[m, at, :] = block
+            s.adjoint[m, at, :] = rounded(block)
 
         return put
 
     def query_back(i, at):
         s.grads[at, :h] = rounded(times_transpose(s.bpr[at, :], s.nw[...]))
-        s.orow[at, :] = rounded(times_transpose(s.hq[at, :], s.no_t[...]))
+        s.grads[at, h : 2 * h] = rounded(times_transpose(s.hq[at, :], s.no_t[...]))
 
     now[2].forward()
     over_tiles(query_back)
@@ -560,7 +588,7 @@
     now[1].forward()
     now[0].gather()
     now[2].relay()
-    scatters[1].fill(product(s.cot_t[...], s.orow[...]))
+    scatters[1].fill(product(s.cot_t[...], s.grads[:, h : 2 * h]))
     now[1].gather()
     now[0].relay()
     now[1].relay()
@@ -568,16 +596,20 @@
     scatters[1].start()
     for m in (2, 0, 1):
         now[m].finish(adjoint_put(m))
-    s.b4[:, :f], s.b4[:, f : 2 * f], s.bow[:, :f] = ns_backward(s)
+    for m in range(COUNT):
+        s.current[m] = s.adjoint[m].astype(f32)
+    ns_backward(s, 0, NS_STEPS - 1)
     scatters[0].forward()
+    ns_backward(s, NS_STEPS - 1, NS_STEPS)
+    s.b4[:, :f], s.b4[:, f : 2 * f], s.bow[:, :f] = ns_finish(s)
 
     def update_back(i, at):
         s.work[:, : 2 * f] = product(s.key[at, :], s.b4[:, : 2 * f])
         s.work[:, 2 * f :] = product(s.scaled[at, :], s.bow[:, :f])
 
         def point(j, col):
-            here = rows_at(j, sub)
-            to = pl.ds(pl.multiple_of(i * tile + j * sub, sub), sub)
+            here = pl.ds(j * sub, sub)
+            to = rows_from(i, j)
             press_in = s.work[here, col : col + half]
             press_up = s.work[here, f + col : f + col + half]
             back_hid = s.work[here, 2 * f + col : 2 * f + col + half]
@@ -597,7 +629,9 @@
 
         over_subs(point)
 
-    over_tiles(update_back)
+    over_tiles(update_back, 0, tiles // 2)
+    scatters[1].forward()
+    over_tiles(update_back, tiles // 2, tiles)
     now = reduces[2]
     now[2].fill(product(s.scaled_t[...], s.hb[:, f:]))
     now[2].start()
@@ -605,7 +639,6 @@
     now[0].start()
     now[1].fill(product(s.key_t[...], s.g4[:, 3 * f :]))
     now[1].start()
-    scatters[1].forward()
 
     def token_back(i, at):
         back_scaled = times_transpose(s.hb[at, :], s.bow[...])
@@ -643,15 +676,15 @@
     over_tiles(inputs_back)
     stores.append(load(s.cot, s.back_hbm, s.store_sems.at[0]))
     now[2].relay()
+    scatters[2].forward()
     now[1].gather()
     now[0].relay()
-    scatters[2].forward()
+    scatters[3].forward()
     now[1].relay()
-    scatters[3].forward()
 
     def sum_put(m):
         def put(at, block):
-            s.totals[m, at, :] = s.adjoint[m, at, :] + block
+            s.totals[m, at, :] = s.adjoint[m, at, :].astype(f32) + block
 
         return put
 

time: 118 us -> 112 us (0.949)
  Pallas kernels: 117 us -> 111 us
    pallas_call x1, Pallas kernels: 114 us -> 108 us  [body(): pl.pallas_call(functools.partial(kernel, n, OPERANDS + RESULTS + tuple(sc...]
where the time goes in v3:
time: 112 us
  Pallas kernels  111 us (99%)
    pallas_call x1, Pallas kernels, body(): pl.pallas_call(functools.partial(kernel, n, OPERANDS + RESULTS + tuple(sc...  108 us
    pallas_call x1, Pallas kernels, body(): pl.pallas_call(functools.partial(copy_kernel, len(outs)), out_shape=[jax....  3 us

profile of v3, /device:TPU:0, one launch (start us, length us, event | category | flops | bytes accessed | tf_op | source)
XLA Modules:
  0.0 112.1 jit_solution(16744438326819756409)
XLA Ops:
  0.6 108.3 %shard_map.169 = (bf16[1024,768]{1,0:T(8,128)(2,1)}, f32[8,128]{1,0:T(8,128)}, f32[256,512]{1,0:T(8,128)}, f32[256,512]{1,0:T(8,128)}, f32[512,256]{1,0:T(8,128)...) custom-call(bf16[1024,768]{1,0:T(8,128)(2,1)} %refs_0_.1, f32[8,128]{1,0:T(8,128)} %bitcast.3, ...), custom_call_target="tpu_custom_call" | custom-call | tf_op jit(solution)/shard_map/pallas_call | solution.py:763
  109.0 3.0 %shard_map.170 = (bf16[1024,768]{1,0:T(8,128)(2,1)}, f32[8,128]{1,0:T(8,128)}, f32[256,512]{1,0:T(8,128)}, f32[256,512]{1,0:T(8,128)}, f32[512,256]{1,0:T(8,128)...) custom-call(bf16[1024,768]{1,0:T(8,128)(2,1)} %get-tuple-element.27.refs_0_, ...), custom_call_target="tpu_custom_call" | custom-call | tf_op jit(solution)/shard_map/pallas_call | solution.py:775

commit v4 on v3

--- a/solution.py
+++ b/solution.py
@@ -560,7 +560,7 @@
 
         over_subs(point)
 
-    over_tiles(query)
+    each_tile(query)
     now = reduces[1]
     now[2].fill(token_sum(s.back_out[...], s.hq[...]))
     now[2].start()
@@ -584,8 +584,8 @@
     over_tiles(query_back)
     now[0].forward()
     now[2].gather()
+    now[1].forward()
     scatters[0].fill(product(s.x_t[...], s.grads[:, :h]))
-    now[1].forward()
     now[0].gather()
     now[2].relay()
     scatters[1].fill(product(s.cot_t[...], s.grads[:, h : 2 * h]))
@@ -629,9 +629,9 @@
 
         over_subs(point)
 
-    over_tiles(update_back, 0, tiles // 2)
+    each_tile(update_back, 0, tiles // 2)
     scatters[1].forward()
-    over_tiles(update_back, tiles // 2, tiles)
+    each_tile(update_back, tiles // 2, tiles)
     now = reduces[2]
     now[2].fill(product(s.scaled_t[...], s.hb[:, f:]))
     now[2].start()
@@ -673,9 +673,9 @@
     def inputs_back(i, at):
         s.cot[at, :] = rounded(times_transpose(s.grads[at, :], s.wall[...]))
 
+    now[2].relay()
     over_tiles(inputs_back)
     stores.append(load(s.cot, s.back_hbm, s.store_sems.at[0]))
-    now[2].relay()
     scatters[2].forward()
     now[1].gather()
     now[0].relay()

time: 112 us -> 111 us (level)
  no operation moved by 1% of the time
where the time goes in v4:
time: 111 us
  Pallas kernels  110 us (99%)
    pallas_call x1, Pallas kernels, body(): pl.pallas_call(functools.partial(kernel, n, OPERANDS + RESULTS + tuple(sc...  107 us
    pallas_call x1, Pallas kernels, body(): pl.pallas_call(functools.partial(copy_kernel, len(outs)), out_shape=[jax....  3 us

profile of v4, /device:TPU:0, one launch (start us, length us, event | category | flops | bytes accessed | tf_op | source)
XLA Modules:
  0.0 111.2 jit_solution(17085568040938536536)
XLA Ops:
  0.6 107.3 %shard_map.169 = (bf16[1024,768]{1,0:T(8,128)(2,1)}, f32[8,128]{1,0:T(8,128)}, f32[256,512]{1,0:T(8,128)}, f32[256,512]{1,0:T(8,128)}, f32[512,256]{1,0:T(8,128)...) custom-call(bf16[1024,768]{1,0:T(8,128)(2,1)} %refs_0_.1, f32[8,128]{1,0:T(8,128)} %bitcast.3, ...), custom_call_target="tpu_custom_call" | custom-call | tf_op jit(solution)/shard_map/pallas_call | solution.py:763
  108.0 3.0 %shard_map.170 = (bf16[1024,768]{1,0:T(8,128)(2,1)}, f32[8,128]{1,0:T(8,128)}, f32[256,512]{1,0:T(8,128)}, f32[256,512]{1,0:T(8,128)}, f32[512,256]{1,0:T(8,128)...) custom-call(bf16[1024,768]{1,0:T(8,128)(2,1)} %get-tuple-element.27.refs_0_, ...), custom_call_target="tpu_custom_call" | custom-call | tf_op jit(solution)/shard_map/pallas_call | solution.py:775
